TPU v7x, 32 devices: a whole 2x2x4 slice. The times are simulated.
32 devices in a mesh: dp: 2 (over core), mp: 4 (over y, x), hidden: 4 (over z).
Axes of the slice: x: 2, y: 2, z: 4, core: 2. Of those that a mesh axis runs over, the one named last changes fastest.
Arguments:
- stored: bfloat16 [768, 32768], P('mp', ('dp', 'hidden')), may hold values from -51 to 51
- positions: int32 [32768], P(('dp', 'hidden')), may hold values from 0 to 1211, as said below
- segments: int32 [32768], P(('dp', 'hidden', 'mp')), may hold values from 0 to 8, as said below
- present: int32 [32768], P(('dp', 'hidden', 'mp')), may hold values from 0 to 1, as said below
- norm_gains: float32 [2, 768], P(None, 'mp'), may hold values from 0.1 to 1.9
- norm_biases: float32 [2, 768], P(None, 'mp'), may hold values from -3 to 3
- input_proj: bfloat16 [768, 3, 768], P('mp', None, 'hidden'), may hold values from -0.3125 to 0.3125
- input_bias: bfloat16 [2, 768], P(None, 'hidden'), may hold values from -3 to 3
- output_proj: bfloat16 [768, 768], P('hidden', 'mp'), may hold values from -0.875 to 0.875
- output_bias: bfloat16 [768], P('mp'), may hold values from -3 to 3
- expand_weight: bfloat16 [768, 3072], P('mp', 'hidden'), may hold values from -0.21875 to 0.21875
- expand_bias: bfloat16 [3072], P('hidden'), may hold values from -3 to 3
- reduce_weight: bfloat16 [768, 3072], P('mp', 'hidden'), may hold values from -0.109375 to 0.109375
- reduce_bias: bfloat16 [768], P('mp'), may hold values from -3 to 3
- cotangent: bfloat16 [768, 32768], P('mp', ('dp', 'hidden')), may hold values from -6 to 6
Outputs:
- output: bfloat16 [768, 32768], P('mp', ('dp', 'hidden'))
- d_stored: float32 [768, 32768], P('mp', ('dp', 'hidden'))
- d_norm_gains: float32 [2, 768], P(None, ('mp', 'dp', 'hidden'))
- d_norm_biases: float32 [2, 768], P(None, ('mp', 'dp', 'hidden'))
- d_input_proj: float32 [768, 3, 768], P(('mp', 'dp'), None, 'hidden')
- d_input_bias: float32 [2, 768], P(None, ('hidden', 'dp'))
- d_output_proj: float32 [768, 768], P(('hidden', 'dp'), 'mp')
- d_output_bias: float32 [768], P(('mp', 'dp'))
- d_expand_weight: float32 [768, 3072], P(('mp', 'dp'), 'hidden')
- d_expand_bias: float32 [3072], P(('hidden', 'dp'))
- d_reduce_weight: float32 [768, 3072], P(('mp', 'dp'), 'hidden')
- d_reduce_bias: float32 [768], P(('mp', 'dp'))
Inputs may be any that keep to these rules, and one draw needn't show every extreme that they name: `segments`: within each packed row of 1024 tokens the clip numbers never fall; every clip but the last of a row holds 128 to 512 tokens; padding tokens carry 8. `present`: padding is the tail of every packed row, 1 to 128 tokens. `positions`: consecutive within a clip; a clip's positions stay below 1212; padding tokens carry 1212 - 1.
All inputs are finite; a program needn't handle non-finite values.
Results may differ from a plain program's by a relative error of at most 0.014.
The roundings to bfloat16 on the way count: a program that leaves them out, or rounds other values in their place, can miss the bound.
Values may be sent and summed in bfloat16 or wider, within the bound.
A program may use at most 384 MiB of HBM per device.

v0:
```python
import functools
import math

import jax
import jax.numpy as jnp
import numpy as np
from jax import lax
from jax.experimental import pallas as pl
from jax.experimental.pallas import tpu as pltpu
from jax.sharding import PartitionSpec as P

D = 768
HEADS = 12
HD = 64
SEQ = 1024
QBB = 1024
PAIR = 2 * HD
PAIRS = HEADS // 2
EPS = 1e-06
MASKED = -1e30
F32 = jnp.float32
BF16 = jnp.bfloat16
VMEM_LIMIT = 60 * 1024 * 1024
PI_2 = (1.5703125, 4.837512969970703125e-4, 7.549789948768648e-8)

NN = (((1,), (0,)), ((), ()))
NT = (((1,), (1,)), ((), ()))


def mm(a, b, dims=NN):
    return lax.dot_general(a, b, dims, preferred_element_type=F32)


def whole(shape):
    return pl.BlockSpec(shape, lambda *_: (0,) * len(shape), pipeline_mode=pl.Buffered(1))


def params(**kw):
    return pltpu.CompilerParams(vmem_limit_bytes=VMEM_LIMIT, **kw)


def lane_sums(x):
    total = x[:, 0:128]
    for j in range(1, x.shape[1] // 128):
        total = total + x[:, j * 128 : (j + 1) * 128]
    return total


def norm_stats(e):
    average = jnp.sum(e, axis=0, keepdims=True) * (1.0 / D)
    spread = jnp.sum(e * e, axis=0, keepdims=True) * (1.0 / D) - average * average
    return average, lax.rsqrt(spread + EPS)


def fill_bias(bias_ref, seg_ref, present_ref):
    seg = seg_ref[...].astype(F32)
    key = jnp.where(present_ref[...] == 1, seg, -1.0)
    key_cols = jnp.broadcast_to(key, (8, SEQ)).T
    for i in range(SEQ // 256):
        same = key_cols[i * 256 : (i + 1) * 256, 0:1] == seg
        row_id = lax.broadcasted_iota(jnp.int32, (256, SEQ), 0) + i * 256
        col_id = lax.broadcasted_iota(jnp.int32, (256, SEQ), 1)
        bias_ref[i * 256 : (i + 1) * 256, :] = jnp.where(same | (row_id == col_id), 0.0, MASKED)


MESH = pl.DeviceIdType.MESH


class Wire:
    def __init__(self, send, recv):
        self.send_sem, self.recv_sem, self.count, self.sent = send, recv, 0, []
        self.me = (lax.axis_index("dp"), lax.axis_index("mp"), lax.axis_index("hidden"))
        self.size = (lax.axis_size("dp"), lax.axis_size("mp"), lax.axis_size("hidden"))

    def peer(self, axis, offset):
        where = list(self.me)
        where[axis] = lax.rem(where[axis] + offset, self.size[axis])
        return tuple(where)

    def origin(self, axis, offset):
        return lax.rem(self.me[axis] - offset + self.size[axis], self.size[axis])

    def meet(self):
        barrier = pltpu.get_barrier_semaphore()
        total = 0
        for axis in range(3):
            for offset in range(1, self.size[axis]):
                pl.semaphore_signal(barrier, 1, device_id=self.peer(axis, offset), device_id_type=MESH)
                total += 1
        pl.semaphore_wait(barrier, total)

    def send(self, src, dst, target):
        copy = pltpu.make_async_remote_copy(
            src, dst, self.send_sem.at[self.count], self.recv_sem.at[self.count], device_id=target, device_id_type=MESH
        )
        copy.start()
        self.count += 1
        self.sent.append(copy)
        return copy

    def keep(self, src, dst):
        copy = pltpu.make_async_copy(src, dst, self.send_sem.at[self.count])
        copy.start()
        self.count += 1
        return copy

    def finish(self):
        assert self.count <= self.send_sem.shape[0], self.count
        for copy in self.sent:
            copy.wait_send()


DP, MP, HID = 0, 1, 2


HALF = D // 2


def sin_cos(angles):
    turns = jnp.floor(angles * (2.0 / math.pi) + 0.5)
    r = ((angles - turns * PI_2[0]) - turns * PI_2[1]) - turns * PI_2[2]
    r2 = r * r
    s = r + r * r2 * (-1.6666654611e-1 + r2 * (8.3321608736e-3 + r2 * -1.9515295891e-4))
    c = 1.0 - 0.5 * r2 + r2 * r2 * (4.166664568298827e-2 + r2 * (-1.388731625493765e-3 + r2 * 2.443315711809948e-5))
    quarter = turns - 4.0 * jnp.floor(turns * 0.25)
    odd = (quarter == 1.0) | (quarter == 3.0)
    flip_s = quarter >= 2.0
    flip_c = (quarter == 1.0) | (quarter == 2.0)
    sine = jnp.where(odd, c, s)
    cosine = jnp.where(odd, s, c)
    return jnp.where(flip_s, -sine, sine), jnp.where(flip_c, -cosine, cosine)


def forward_kernel(
    x_ref, c_ref, w1a_ref, w1b_ref, w2_ref, we_ref, wr_ref, cols_ref, rows_ref, pos_ref, rate_ref, seg_ref, present_ref,
    et_out, ft_out, w1_out, qkv_out, out_out, dmid_out, do_out, near_r, near_e, last_sum, wef_ref, wrf_ref,
    lse_ref, p_ref, dbe_ref, dw2_ref, dbf_ref, dgs_ref,
    xt, ct, w1af, w1bf, w2f, rowsf, colsf, rates, tab, et, ft, f, w1, qkv, bias, vt, wb, at, out, wblk, dblk, w2c, theirs, sums,
    send, recv, z_send, z_recv, p_send, p_recv, c_send, c_recv, x_send, x_recv, n_send, n_recv, o_sem, local,
):
    wire = Wire(send, recv)
    d, m, h = wire.me
    dp, mp, hid = wire.size
    rows = D // mp
    wide = D // hid
    fcols = we_ref.shape[1]
    half = rows // dp
    offset = pl.multiple_of(d * half, half)
    half2 = wide // dp
    w2_part = w2_ref
    if w2_ref.shape[0] > half2:
        w2_part = w2_ref.at[pl.ds(pl.multiple_of(d * half2, half2), half2)]
    own = (
        (w1a_ref, lambda mm_, hh: w1af.at[hh, mm_, d], lambda: w1af.at[:, :, d], HID),
        (w1b_ref, lambda mm_, hh: w1bf.at[hh, mm_, d], lambda: w1bf.at[:, :, d], MP),
        (w2_part, lambda mm_, hh: w2f.at[mm_, hh, d], lambda: w2f.at[:, :, d], HID),
    )
    wire.meet()
    waits, stored = [], []
    first, second, third = {}, {}, {}

    def swap(src_ref, dst_ref):
        mine = pl.ds(pl.multiple_of(m * rows, rows), rows)
        moved = []
        for q in range(1, mp):
            to = wire.peer(MP, q)
            moved.append(wire.send(src_ref.at[:, pl.ds(pl.multiple_of(to[1] * SEQ, SEQ), SEQ)], dst_ref.at[mine], to))
        return moved, wire.keep(src_ref.at[:, pl.ds(pl.multiple_of(m * SEQ, SEQ), SEQ)], dst_ref.at[mine])

    def landed(pair):
        for copy in pair[0]:
            copy.wait_recv()
        pair[1].wait()

    def stage_one(i):
        src, dst, _, axis = own[i]
        first[i] = [wire.keep(src, dst(m, h))]
        first[i] += [wire.send(src, dst(m, h), wire.peer(axis, o)) for o in range(1, wire.size[axis])]

    def stage_two(i):
        _, dst, _, axis = own[i]
        other = MP if axis == HID else HID
        second[i] = []
        for o, copy in enumerate(first[i]):
            if o == 0:
                copy.wait()
            else:
                copy.wait_recv()
            at_ = wire.origin(axis, o)
            piece = dst(m, at_) if axis == HID else dst(at_, h)
            second[i] += [wire.send(piece, piece, wire.peer(other, q)) for q in range(1, wire.size[other])]

    def stage_three(i):
        for copy in second[i]:
            copy.wait_recv()
        third[i] = [wire.send(own[i][2](), own[i][2](), wire.peer(DP, r)) for r in range(1, dp)]

    def done(i):
        for copy in third[i]:
            copy.wait_recv()

    full = (wef_ref, wrf_ref)
    part = (we_ref.at[pl.ds(offset, half)], wr_ref.at[pl.ds(offset, half)])
    whole_planes = ((1,), (1, hid - 1))
    order = [0, 1, hid - 1] + list(range(2, hid - 1))

    def plane_of(o):
        return lax.rem(h - o + hid, hid)

    def piece(j, mm_, dd, o):
        at_ = pl.ds(pl.multiple_of(mm_ * rows + dd * half, half), half)
        return full[j].at[at_, pl.ds(pl.multiple_of(plane_of(o) * fcols, fcols), fcols)]

    def remote(src, dst, sems, target):
        return pltpu.make_async_remote_copy(src, dst, sems[0], sems[1], device_id=target, device_id_type=MESH)

    def to_plane(j, o, q):
        src = part[j] if o == 0 else piece(j, m, d, o)
        return remote(src, piece(j, m, d, o), (p_send.at[j, o, q], p_recv.at[j, o, q]), wire.peer(MP, q))

    def to_depth(j, o, k):
        if o in whole_planes[j]:
            src = dst = piece(j, k, d, 0)
        else:
            src, dst = part[j], piece(j, m, d, 0)
        return remote(src, dst, (z_send.at[j, o, k], z_recv.at[j, o, k]), wire.peer(HID, o))

    def depth_count(j, o):
        return mp if o in whole_planes[j] else 1

    def to_core(j, o, k, r):
        return remote(
            piece(j, k, d, o), piece(j, k, d, o), (c_send.at[j, o, k, r - 1], c_recv.at[j, o, k, r - 1]), wire.peer(DP, r)
        )

    def keep_own(j):
        return pltpu.make_async_copy(part[j], piece(j, m, d, 0), local.at[j])

    def plane_start(j, o):
        if o:
            to_depth(j, o, 0).wait_recv()
        else:
            keep_own(j).start()
        for q in range(1, mp):
            to_plane(j, o, q).start()

    def plane_wait(j, o):
        if o == 0:
            keep_own(j).wait()
        for q in range(1, mp):
            to_plane(j, o, q).wait_recv()

    def depth_start(j, o):
        for k in range(depth_count(j, o)):
            to_depth(j, o, k).start()

    def apart(j):
        return [o for o in range(1, hid) if o not in whole_planes[j]]

    def core_start(j, o):
        if o in whole_planes[j]:
            for k in range(mp):
                to_depth(j, o, k).wait_recv()
        elif o:
            plane_wait(j, o)
        for k in range(mp):
            for r in range(1, dp):
                to_core(j, o, k, r).start()

    def arrived(j, o):
        for k in range(mp):
            for r in range(1, dp):
                to_core(j, o, k, r).wait_recv()

    small = [wire.send(cols_ref, colsf.at[m], wire.peer(MP, q)) for q in range(1, mp)]
    small += [wire.send(rows_ref, rowsf.at[h], wire.peer(HID, o)) for o in range(1, hid)]
    kept = [wire.keep(cols_ref, colsf.at[m]), wire.keep(rows_ref, rowsf.at[h])]
    stage_one(0)
    stage_one(1)
    x_in = swap(x_ref, xt)

    rates[...] = jnp.broadcast_to(rate_ref[...], (8, HALF)).T
    places = pos_ref[:, pl.ds(pl.multiple_of(m * SEQ, SEQ), SEQ)].astype(F32)

    def table_rows(j, _):
        at_ = pl.ds(pl.multiple_of(j * 64, 64), 64)
        sine, cosine = sin_cos(rates[at_, 0:1] * places)
        tab[at_, :] = sine
        tab[pl.ds(pl.multiple_of(j * 64 + HALF, 64), 64), :] = cosine
        return 0

    lax.fori_loop(0, 1, table_rows, 0)
    stage_two(0)
    stage_two(1)
    lax.fori_loop(1, HALF // 64, table_rows, 0)
    fill_bias(bias, seg_ref, present_ref)
    for copy in small:
        copy.wait_recv()
    for copy in kept:
        copy.wait()
    for mm_ in range(mp):
        p_ref[mm_ * rows : (mm_ + 1) * rows, 0:8] = colsf[mm_].T[:rows, :]
    wb[...] = jnp.zeros_like(wb)
    for hh in range(hid):
        wb[:, hh * wide : (hh + 1) * wide] = rowsf[hh, 1:2, :wide]
        wb[:, 2 * D + hh * wide : 2 * D + (hh + 1) * wide] = rowsf[hh, 2:3, :wide]
    landed(x_in)

    def norm_cols(j, _):
        cols = pl.ds(pl.multiple_of(j * 256, 256), 256)
        e = xt[:, cols].astype(F32) + tab[:, cols]
        et[:, cols] = e
        average, inv = norm_stats(e)
        low = ((e - average) * inv * p_ref[:, 0:1] + p_ref[:, 1:2]).astype(BF16)
        ft[:, cols] = low
        f[cols, :] = low.T
        return 0

    lax.fori_loop(0, SEQ // 256, norm_cols, 0)
    stored += [wire.keep(et, et_out), wire.keep(ft, ft_out)]
    stage_three(0)
    stage_three(1)
    for j in (1, 0):
        for o in apart(j):
            depth_start(j, o)
    plane_start(1, 0)
    stage_one(2)
    plane_start(0, 0)
    c_in = swap(c_ref, ct)
    def unpack(dd):
        for hh in range(hid):
            for mm_ in range(mp):
                at_ = slice(mm_ * rows + dd * half, mm_ * rows + (dd + 1) * half)
                for k in range(3):
                    if k < 2:
                        value = w1af[hh, mm_, dd, :, k * wide : (k + 1) * wide]
                    else:
                        value = w1bf[hh, mm_, dd]
                    w1[at_, k * D + hh * wide : k * D + (hh + 1) * wide] = value

    if dp == 2:
        for dd in range(dp):

            @pl.when(d == dd)
            def _():
                unpack(dd)

        done(0)
        done(1)
        for dd in range(dp):

            @pl.when(d == 1 - dd)
            def _():
                unpack(dd)

    else:
        done(0)
        done(1)
        for dd in range(dp):
            unpack(dd)
    stored.append(wire.keep(w1, w1_out))

    def cols_of(n, scale):
        cols = pl.ds(pl.multiple_of(n * 256, 256), 256)
        y = (mm(f[...], w1[:, cols]) + wb[:, cols]).astype(BF16)
        qkv[:, cols] = y * jnp.asarray(scale, BF16)
        return 0

    lax.fori_loop(0, D // 256, lambda n, c: cols_of(n, HD**-0.5), 0)
    stage_two(2)
    plane_wait(1, 0)
    for o in whole_planes[1]:
        depth_start(1, o)
    lax.fori_loop(D // 256, 3 * D // 256, lambda n, c: cols_of(n, 1.0), 0)
    stored.append(wire.keep(qkv, qkv_out))

    low = lax.broadcasted_iota(jnp.int32, (SEQ, PAIR), 1) < HD
    lse_ref[...] = jnp.zeros_like(lse_ref)

    def pair_of(p, _):
        lanes = pl.ds(pl.multiple_of(p * PAIR, PAIR), PAIR)
        k_lanes = pl.ds(pl.multiple_of(p * PAIR + D, PAIR), PAIR)
        v_lanes = pl.ds(pl.multiple_of(p * PAIR + 2 * D, PAIR), PAIR)
        vt[...] = qkv[:, v_lanes].T
        q = qkv[:, lanes]
        for hh in range(2):
            qm = jnp.where(low if hh == 0 else ~low, q, jnp.zeros_like(q))
            s = mm(qkv[:, k_lanes], qm, NT) + bias[...]
            top = jnp.max(s, axis=0, keepdims=True)
            e = jnp.exp(s - top)
            total = jnp.sum(e, axis=0, keepdims=True)
            o = mm(vt[hh * HD : (hh + 1) * HD, :], e.astype(BF16)) / total
            at[pl.ds(pl.multiple_of(p * PAIR + hh * HD, HD), HD), :] = o.astype(BF16)
            lse_ref[p, hh : hh + 1, :] = top + jnp.log(total)
        return 0

    lax.fori_loop(0, PAIRS // 3, pair_of, 0)
    plane_wait(0, 0)
    for o in whole_planes[0]:
        depth_start(0, o)
    for j in (1, 0):
        for o in apart(j):
            plane_start(j, o)
    lax.fori_loop(PAIRS // 3, 2 * PAIRS // 3, pair_of, 0)
    stage_three(2)
    for j in range(2):
        core_start(j, 0)
    lax.fori_loop(2 * PAIRS // 3, PAIRS, pair_of, 0)
    for copy in stored:
        copy.wait()
    landed(c_in)
    done(2)

    ot, ds_sum, st, bt, mid = bias.at[pl.ds(0, D)], tab, xt, ft, et
    tokens = [pl.ds(n * D, D) for n in range(3)]
    for mm_ in range(mp):
        for hh in range(hid):
            for dd in range(dp):
                at_ = hh * wide + dd * (wide // dp)
                w2c[at_ : at_ + wide // dp, mm_ * rows : (mm_ + 1) * rows] = w2f[mm_, hh, dd]
    w2t = w2c[...].T

    def middle_cols(j, _):
        cols = pl.ds(pl.multiple_of(j * 256, 256), 256)
        value = et[:, cols] + (mm(w2t, at[:, cols]) + p_ref[:, 4:5])
        mid[:, cols] = value
        ot[:, cols] = value + p_ref[:, 5:6]
        average, inv = norm_stats(value)
        s = ((value - average) * inv * p_ref[:, 2:3] + p_ref[:, 3:4]).astype(BF16)
        st[:, cols] = s
        qkv[cols, tokens[0]] = s.T
        qkv[cols, tokens[1]] = ct[:, cols].T
        return 0

    lax.fori_loop(0, SEQ // 256, middle_cols, 0)
    ds_sum[...] = jnp.zeros_like(ds_sum)

    def fetch(j, o):
        hcols = pl.ds(pl.multiple_of(plane_of(o) * fcols, fcols), fcols)
        return pltpu.make_async_copy(full[j].at[:, hcols], wblk.at[j], local.at[2 + j])

    def place(n):
        o = 0
        for k in range(1, hid):
            o = jnp.where(n == k, order[k], o)
        return o

    def swap_core(j, n, k, r):
        to = wire.peer(DP, r)
        return remote(
            dblk.at[j, k, to[0]], theirs.at[lax.rem(n, 2), j, r - 1, k], (x_send.at[j, n, k, r - 1], x_recv.at[j, n, k, r - 1]), to
        )

    def each_core(n, do):
        for j in range(2):
            for k in range(mp):
                for r in range(1, dp):
                    do(swap_core(j, n, k, r))

    end = hid - 1

    def sum_depth(n):
        to = (d, m, plane_of(place(n)))
        return remote(sums.at[lax.rem(n, 2), 0], near_r.at[n], (n_send.at[n, 0], n_recv.at[n, 0]), to)

    def sum_plane(n, q):
        to = wire.peer(MP, q)
        return remote(sums.at[lax.rem(n, 2), 1, to[1]], near_e.at[n, q], (n_send.at[n, q], n_recv.at[n, q]), to)

    def save(j, n, last):
        slot = lax.rem(n, 2)
        if last:
            return pltpu.make_async_copy(sums.at[slot, j], last_sum.at[j], o_sem.at[j, n])
        if j == 0:
            return pltpu.make_async_copy(sums.at[0, 0], near_r.at[0], o_sem.at[0, 0])
        return pltpu.make_async_copy(sums.at[slot, 1, m], near_e.at[n, 0], o_sem.at[1, n])

    def add_cores(n, last=False):
        each_core(n, lambda copy: copy.wait_recv())
        slot = lax.rem(n, 2)
        for j in range(2):
            for k in range(mp):
                value = dblk[j, k, d].astype(F32)
                for r in range(1, dp):
                    value = value + theirs[slot, j, r - 1, k].astype(F32)
                sums[slot, j, k] = value.astype(BF16)
        if last:
            for j in range(2):
                save(j, n, True).start()
            return
        for q in range(1, mp):
            sum_plane(n, q).start()
        save(1, n, False).start()

    def gone(n):
        for q in range(1, mp):
            sum_plane(n, q).wait_send()
        save(1, n, False).wait()

    def block(n, _):
        o = place(n)
        hh = plane_of(o)
        for j in range(2):
            arrived(j, o)
        for j in range(2):
            fetch(j, o).start()
        for j in range(2):
            fetch(j, o).wait()

        pre = mm(qkv[:, tokens[0]], wblk[0]) + rowsf[hh, 0:1, :]
        cdf = 0.5 * (1.0 + lax.erf(pre * (1.0 / math.sqrt(2.0))))
        act = (pre * cdf).astype(BF16)
        slope = cdf + pre * jnp.exp(-0.5 * pre * pre) * (1.0 / math.sqrt(2.0 * math.pi))
        grad = (mm(qkv[:, tokens[1]], wblk[1]) * slope).astype(BF16)

        @pl.when(n == 3)
        def _():
            gone(0)
            save(0, 0, False).wait()

        @pl.when(n > 3)
        def _():
            gone(n - 3)
            sum_depth(n - 3).wait_send()

        @pl.when(n > 0)
        def _():
            add_cores(n - 1)
            each_core(n - 1, lambda copy: copy.wait_send())

        @pl.when(n == 1)
        def _():
            save(0, 0, False).start()

        @pl.when(n > 1)
        def _():
            sum_depth(n - 1).start()

        for j, value in enumerate((mm(ct[...], act), mm(st[...], grad))):
            for k in range(mp):
                for dd in range(dp):
                    at_ = k * rows + dd * half
                    dblk[j, k, dd] = value[at_ : at_ + half, :].astype(BF16)
        each_core(n, lambda copy: copy.start())
        dbe_ref[hh, 0:1, :] = jnp.sum(grad.astype(F32), axis=0, keepdims=True)
        ot[...] += mm(wblk[1], act, NT)
        ds_sum[...] += mm(wblk[0], grad, NT)

        for k in range(1, hid):

            @pl.when(n + 1 == k)
            def _():
                for j in range(2):
                    core_start(j, order[k])

        return 0

    lax.fori_loop(0, hid, block, 0)
    gone(end - 2)
    sum_depth(end - 2).wait_send()
    add_cores(end, True)
    dgs_ref[...] = jnp.zeros_like(dgs_ref)

    def back_cols(j, _):
        cols = pl.ds(pl.multiple_of(j * 256, 256), 256)
        value = mid[:, cols]
        out[:, cols] = ot[:, cols].astype(BF16)
        average, inv = norm_stats(value)
        normed = (value - average) * inv
        ds = ds_sum[:, cols]
        scaled = ds * p_ref[:, 2:3]
        total = jnp.sum(scaled, axis=0, keepdims=True) * (1.0 / D)
        crossed = jnp.sum(scaled * normed, axis=0, keepdims=True) * (1.0 / D)
        dmid = ct[:, cols].astype(F32) + inv * (scaled - total - normed * crossed)
        mid[:, cols] = dmid
        low_ = dmid.astype(BF16)
        bt[:, cols] = low_
        qkv[cols, tokens[2]] = mm(w2c[...], low_).astype(BF16).T
        dgs_ref[0] += lane_sums(ds * normed)
        dgs_ref[1] += lane_sums(ds)
        return 0

    lax.fori_loop(0, SEQ // 256, back_cols, 0)
    last = [wire.keep(out, out_out), wire.keep(mid, dmid_out), wire.keep(qkv.at[:, tokens[2]], do_out)]
    ones = jnp.ones((8, SEQ), BF16)
    dbf_ref[0] = mm(ones, ct[...], NT)
    dbf_ref[1] = mm(ones, bt[...], NT)
    for j in range(mp):
        dw2_ref[j] = mm(at[...], bt[j * rows : (j + 1) * rows, :], NT).astype(BF16)
    each_core(end, lambda copy: copy.wait_send())
    gone(end - 1)
    sum_depth(end - 1).wait_send()
    for j in range(2):
        save(j, end, True).wait()
    for n in range(end):
        if n:
            sum_depth(n).wait_recv()
        for q in range(1, mp):
            sum_plane(n, q).wait_recv()
    for copy in last:
        copy.wait()
    wire.finish()
    for j in range(2):
        for o in range(hid):
            if o:
                for k in range(depth_count(j, o)):
                    to_depth(j, o, k).wait_send()
            if o not in whole_planes[j]:
                for q in range(1, mp):
                    to_plane(j, o, q).wait_send()
            for k in range(mp):
                for r in range(1, dp):
                    to_core(j, o, k, r).wait_send()


def forward(x, c, w1a, w1b, w2, we, wr, cols, rows, pos, rate, seg, present):
    dp, mp, hid = lax.axis_size("dp"), lax.axis_size("mp"), lax.axis_size("hidden")
    half = D // mp // dp
    fc = we.shape[1]
    ff = hid * fc
    sds = jax.ShapeDtypeStruct
    out_shape = (
        sds((D, SEQ), F32), sds((D, SEQ), BF16), sds((D, 3 * D), BF16), sds((SEQ, 3 * D), BF16),
        sds((D, SEQ), BF16), sds((D, SEQ), F32), sds((SEQ, D), BF16), sds((hid - 1, mp, half, fc), BF16),
        sds((hid - 1, mp, half, fc), BF16), sds((2, mp, half, fc), BF16), sds((D, ff), BF16), sds((D, ff), BF16),
        sds((PAIRS, 8, SEQ), F32), sds((D, 128), F32), sds((hid, 8, fc), F32), sds((mp, D, D // mp), BF16),
        sds((2, 8, D), F32), sds((2, D, 128), F32),
    )
    n = (mp - 1) + (hid - 1) + 2 + 2 * hid + mp + 2 * hid * (mp - 1) + mp * (hid - 1) + 3 * (dp - 1) + 2 * mp + 7
    hbm = pl.BlockSpec(memory_space=pl.ANY)
    vmem = pl.BlockSpec(memory_space=pltpu.VMEM)
    vm = lambda dtype, *shape: pltpu.VMEM(shape, dtype)
    sem = lambda *shape: pltpu.SemaphoreType.DMA(shape)
    return pl.pallas_call(
        forward_kernel,
        out_shape=out_shape,
        in_specs=[hbm] * 9 + [vmem] * 4,
        out_specs=(hbm,) * 12 + (vmem,) * 6,
        scratch_shapes=[
            vm(BF16, D, SEQ), vm(BF16, D, SEQ), vm(BF16, hid, mp, dp, half, w1a.shape[1]),
            vm(BF16, hid, mp, dp, half, w1b.shape[1]), vm(BF16, mp, hid, dp, D // hid // dp, w2.shape[1]), vm(F32, hid, *rows.shape),
            vm(F32, mp, *cols.shape), vm(F32, HALF, 8),
            vm(F32, D, SEQ), vm(F32, D, SEQ), vm(BF16, D, SEQ), vm(BF16, SEQ, D), vm(BF16, D, 3 * D),
            vm(BF16, SEQ, 3 * D), vm(F32, SEQ, SEQ), vm(BF16, PAIR, SEQ), vm(F32, 1, 3 * D),
            vm(BF16, D, SEQ), vm(BF16, D, SEQ), vm(BF16, 2, D, fc), vm(BF16, 2, mp, dp, half, fc), vm(BF16, D, D),
            vm(BF16, 2, 2, dp - 1, mp, half, fc), vm(BF16, 2, 2, mp, half, fc),
            sem(n), sem(n), sem(2, hid, mp), sem(2, hid, mp), sem(2, hid, mp), sem(2, hid, mp),
            sem(2, hid, mp, dp - 1), sem(2, hid, mp, dp - 1), sem(2, hid, mp, dp - 1), sem(2, hid, mp, dp - 1),
            sem(hid, mp), sem(hid, mp), sem(2, hid), sem(4),
        ],
        compiler_params=params(collective_id=0, has_side_effects=True),
        name="forward",
    )(x, c, w1a, w1b, w2, we, wr, cols, rows, pos, rate, seg, present)


def backward_kernel(
    o_ref, dw2_ref, near_r, near_e, last_sum, qkv_in, do_in, lse_ref, seg_ref, present_ref, ft_in, w_in, et_in, dmid_in, p_ref,
    dbe_ref, dbf_ref, dgs_ref,
    of_ref, xf_ref, g1_ref, g2_ref, ge_ref, gr_ref, vecf_ref,
    qkv, do, bias, kt, dqt, dk, dv, dka, dva, ft, et, dmid, dgp,
    a0, a1, a2, o0, o1, s2, b0, b1, b2, be, br, t0, t1, t2, t3, t4, c0, c1, c2, c3, c4,
    v0, va, vb, vc, v1, v2, loads, send, recv,
):
    wire = Wire(send, recv)
    d, m, h = wire.me
    dp, mp, hid = wire.size
    rows = D // mp
    wide = D // hid
    half = rows // dp
    fcols = ge_ref.shape[1]
    v_in = (va, vb, vc)
    slab0 = o0.shape[1:]
    hslice = lambda hh: pl.ds(pl.multiple_of(hh * fcols, fcols), fcols)

    def load(n, src, dst):
        copy = pltpu.make_async_copy(src, dst, loads.at[n])
        copy.start()
        return copy

    parts = []
    for p in range(PAIRS):
        got = []
        for k in range(3):
            lanes = slice(k * D + p * PAIR, k * D + (p + 1) * PAIR)
            got.append(load(4 * p + k, qkv_in.at[:, lanes], qkv.at[:, lanes]))
        lanes = slice(p * PAIR, (p + 1) * PAIR)
        got.append(load(4 * p + 3, do_in.at[:, lanes], do.at[:, lanes]))
        parts.append(got)
    others = [load(4 * PAIRS + i, a, b) for i, (a, b) in enumerate(((ft_in, ft), (et_in, et), (dmid_in, dmid)))]
    wire.meet()
    items = (
        (lambda dd: o0.at[dd], a0, o0.at[d], b0, t0, c0, None, MP, HID),
        (lambda dd: o1.at[dd], a1, o1.at[d], b1, t1, c1, None, HID, HID),
        (lambda dd: dw2_ref.at[:, :, dd], a2, s2, b2, t2, c2, g2_ref, MP, MP),
        (None, None, None, be, t3, c3, ge_ref, MP, None),
        (None, None, None, br, t4, c4, gr_ref, HID, None),
    )
    core, kept, near, far = {}, {}, {}, {}
    end = hid - 1
    plane = lambda o: lax.rem(h - o + hid, hid)
    order = [0, 1, hid - 1] + list(range(2, hid - 1))
    at = 4 * PAIRS + 4
    own = {
        4: [load(at, near_r, br.at[pl.ds(0, end)])],
        3: [load(at + 1 + n, near_e.at[n], be.at[:, :, hslice(plane(order[n]))]) for n in range(end)],
    }
    own[3].append(load(at + 1 + end, last_sum.at[1, m], be.at[0, :, hslice(plane(order[end]))]))

    def stage_core(i):
        src, a, s = items[i][:3]
        core[i] = [wire.send(src(wire.peer(DP, r)[0]), a.at[r - 1], wire.peer(DP, r)) for r in range(1, dp)]
        if i > 1:
            kept[i] = wire.keep(src(d), s)

    def add_all(dst, own, others, shape):
        lead = shape[:-2]

        def body(n, _):
            index = []
            for size in reversed(lead):
                index.insert(0, lax.rem(n, size))
                n = lax.div(n, size)
            index = tuple(index)
            value = own[index].astype(F32)
            for j in range(others.shape[0]):
                value = value + others[(j,) + index].astype(F32)
            dst[index] = value.astype(dst.dtype)
            return 0

        lax.fori_loop(0, math.prod(lead), body, 0)

    def part(i, ref, axis, at, leads):
        if items[i][8] is None:
            return ref.at[(slice(None),) * len(leads) + (slice(None), hslice(at))] if axis == HID else ref.at[at]
        return ref.at[at] if leads[0] == axis else ref.at[:, at]

    def leads_of(i):
        lead = items[i][8]
        return (MP,) if lead is None else ((HID, MP) if lead == HID else (MP, HID))

    def stage_near(i):
        if i == 4:
            near[4] = [wire.send(last_sum.at[0], br.at[end], wire.peer(HID, hid - order[end]))]
            return
        if i == 3:
            here = hslice(plane(order[end]))
            near[3] = []
            for q in range(1, mp):
                to = wire.peer(MP, q)
                near[3].append(wire.send(last_sum.at[1, to[1]], be.at[q, :, here], to))
            return
        _, a, s, b, t, c, g, axis, _ = items[i]
        for copy in core[i]:
            copy.wait_recv()
        if i in kept:
            kept[i].wait()
        add_all(s, s, a, s.shape)
        near[i] = [
            wire.send(part(i, s, axis, wire.peer(axis, q)[axis], leads_of(i)), b.at[q - 1], wire.peer(axis, q))
            for q in range(1, wire.size[axis])
        ]

    def stage_far(i):
        _, a, s, b, t, c, g, axis, lead = items[i]
        if i < 3:
            for copy in near[i] if i else nears_half[0] + nears_half[1]:
                copy.wait_recv()
            add_all(t, part(i, s, axis, wire.me[axis], leads_of(i)), b, t.shape)
        else:
            for copy in near[i]:
                copy.wait_recv()
            for copy in own[i]:
                copy.wait()
            add_all(t, b.at[0], b.at[pl.ds(1, b.shape[0] - 1)], t.shape)
        other = MP if axis == HID else HID
        left = tuple(x for x in leads_of(i) if x != axis)
        far[i] = []
        for q in range(1, wire.size[other]):
            to = wire.peer(other, q)
            far[i].append(wire.send(part(i, t, other, to[other], left), c.at[q - 1], to))

    def stage_end(i):
        _, a, s, b, t, c, g, axis, lead = items[i]
        other = MP if axis == HID else HID
        left = tuple(x for x in leads_of(i) if x != axis)
        for copy in far[i]:
            copy.wait_recv()
        value = part(i, t, other, wire.me[other], left)[...].astype(F32)
        for j in range(c.shape[0]):
            value = value + c[j].astype(F32)
        if i == 0:
            g1_ref[0] = value[:, :wide]
            g1_ref[1] = value[:, wide:]
        elif i == 1:
            g1_ref[2] = value
        else:
            g[...] = value

    moved, held = [], []

    def swap(src_ref, dst_ref):
        mine = pl.ds(pl.multiple_of(m * SEQ, SEQ), SEQ)
        for q in range(1, mp):
            to = wire.peer(MP, q)
            moved.append(wire.send(src_ref.at[pl.ds(pl.multiple_of(to[1] * rows, rows), rows)], dst_ref.at[:, mine], to))
        held.append(wire.keep(src_ref.at[pl.ds(pl.multiple_of(m * rows, rows), rows)], dst_ref.at[:, mine]))

    vec = {}

    def vec_send(axis, src):
        vec[axis] = [wire.send(src, v_in[axis].at[o - 1], wire.peer(axis, o)) for o in range(1, wire.size[axis])]

    def vec_sum(axis, src, dst):
        for copy in vec[axis]:
            copy.wait_recv()
        total = src[...]
        for j in range(wire.size[axis] - 1):
            total = total + v_in[axis][j]
        dst[...] = total

    stage_near(4)
    stage_near(3)
    stage_core(2)
    swap(o_ref, of_ref)
    fill_bias(bias, seg_ref, present_ref)
    low = lax.broadcasted_iota(jnp.int32, (QBB, PAIR), 1) < HD

    def pair_of(p, _):
        off = pl.multiple_of(p * PAIR, PAIR)
        lanes = pl.ds(off, PAIR)
        k_lanes = pl.ds(pl.multiple_of(off + D, PAIR), PAIR)
        v_lanes = pl.ds(pl.multiple_of(off + 2 * D, PAIR), PAIR)
        kt[...] = qkv[:, k_lanes].T
        dka[...] = jnp.zeros_like(dka)
        dva[...] = jnp.zeros_like(dva)

        def block(j, _):
            cols = pl.ds(pl.multiple_of(j * QBB, QBB), QBB)
            q = qkv[cols, lanes]
            g = do[cols, lanes]
            for hh in range(2):
                keep = low if hh == 0 else ~low
                qm = jnp.where(keep, q, jnp.zeros_like(q))
                gm = jnp.where(keep, g, jnp.zeros_like(g))
                e = jnp.exp(mm(qkv[:, k_lanes], qm, NT) + bias[:, cols] - lse_ref[p, hh : hh + 1, cols])
                t = e * mm(qkv[:, v_lanes], gm, NT)
                ds = (t - e * jnp.sum(t, axis=0, keepdims=True)).astype(BF16)
                dva[...] += mm(e.astype(BF16), gm)
                dka[...] += mm(ds, qm)
                dq = mm(kt[hh * HD : (hh + 1) * HD, :], ds) * HD**-0.5
                dqt[pl.ds(pl.multiple_of(off + hh * HD, HD), HD), cols] = dq.astype(BF16)
            return 0

        lax.fori_loop(0, SEQ // QBB, block, 0)
        dk[:, lanes] = dka[...].astype(BF16)
        dv[:, lanes] = dva[...].astype(BF16)
        return 0

    def pairs(first, last):
        for p in range(first, last):
            for copy in parts[p]:
                copy.wait()
        lax.fori_loop(first, last, pair_of, 0)

    span = D // 2
    each = hid // 2

    def weight_half(g):
        wide_k = mm(ft[...], dk[:, g * span : (g + 1) * span]).astype(BF16)
        wide_v = mm(ft[...], dv[:, g * span : (g + 1) * span]).astype(BF16)
        for hh in range(g * each, (g + 1) * each):
            lanes = slice((hh - g * each) * wide, (hh - g * each + 1) * wide)
            value_q = mm(ft[...], dqt[hh * wide : (hh + 1) * wide, :], NT).astype(BF16)
            for mm_ in range(mp):
                for dd in range(dp):
                    at_ = slice(mm_ * rows + dd * half, mm_ * rows + (dd + 1) * half)
                    o0[dd, hh, mm_, :, 0:wide] = value_q[at_, :]
                    o0[dd, hh, mm_, :, wide : 2 * wide] = wide_k[at_, lanes]
                    o1[dd, hh, mm_] = wide_v[at_, lanes]

    cores_half, nears_half = {}, {}

    def core_half(g):
        hs = pl.ds(g * each, each)
        cores_half[g] = [
            wire.send(o0.at[wire.peer(DP, r)[0], hs], a0.at[r - 1, hs], wire.peer(DP, r)) for r in range(1, dp)
        ]

    def near_half(g):
        hs = pl.ds(g * each, each)
        for copy in cores_half[g]:
            copy.wait_recv()
        add_all(o0.at[d, hs], o0.at[d, hs], a0.at[:, hs], (each,) + slab0[1:])
        nears_half[g] = []
        for q in range(1, mp):
            to = wire.peer(MP, q)
            nears_half[g].append(wire.send(o0.at[d, hs, to[1]], b0.at[q - 1, hs], to))

    pairs(0, PAIRS // 2)
    stage_near(2)
    for copy in others:
        copy.wait()
    weight_half(0)
    core_half(0)
    pairs(PAIRS // 2, PAIRS // 2 + 1)
    near_half(0)
    pairs(PAIRS // 2 + 1, PAIRS)
    w1 = qkv.at[pl.ds(0, D)]
    w_load = load(4 * PAIRS + 3, w_in, w1)
    weight_half(1)
    stage_core(1)
    core_half(1)
    df = bias.at[pl.ds(0, D)]
    w_load.wait()
    dx = ft

    def feature_cols(j, _):
        cols = pl.ds(pl.multiple_of(j * 256, 256), 256)
        value = mm(w1[:, 0:D], dqt[:, cols])
        value += mm(w1[:, D : 2 * D], dk[cols, :], NT)
        value += mm(w1[:, 2 * D : 3 * D], dv[cols, :], NT)
        df[:, cols] = value
        return 0

    lax.fori_loop(0, SEQ // 256, feature_cols, 0)
    stage_near(1)
    near_half(1)
    dgp[...] = jnp.zeros_like(dgp)

    def norm_cols(j, _):
        cols = pl.ds(pl.multiple_of(j * 256, 256), 256)
        e = et[:, cols]
        average, inv = norm_stats(e)
        normed = (e - average) * inv
        g = df[:, cols]
        scaled = g * p_ref[:, 0:1]
        total = jnp.sum(scaled, axis=0, keepdims=True) * (1.0 / D)
        crossed = jnp.sum(scaled * normed, axis=0, keepdims=True) * (1.0 / D)
        dx[:, cols] = (dmid[:, cols] + inv * (scaled - total - normed * crossed)).astype(BF16)
        dgp[0] += lane_sums(g * normed)
        dgp[1] += lane_sums(g)
        return 0

    lax.fori_loop(0, SEQ // 256, norm_cols, 0)
    swap(dx, xf_ref)
    for i in (3, 2, 4):
        stage_far(i)
    ones = jnp.ones((8, SEQ), BF16)
    v0[...] = jnp.zeros_like(v0)
    for n in range(2):
        v0[n : n + 1, :] = jnp.sum(dgp[n].T, axis=0, keepdims=True)
        v0[2 + n : 3 + n, :] = jnp.sum(dgs_ref[n].T, axis=0, keepdims=True)
        v0[6 + n : 7 + n, :] = dbf_ref[n, 0:1, :]
    v0[4:5, :] = mm(ones, dqt[...], NT)[0:1]
    v0[5:6, :] = mm(ones, dv[...])[0:1]
    for hh in range(hid):
        row, lane = divmod(hh * fcols, D)
        v0[8 + row : 9 + row, lane : lane + fcols] = dbe_ref[hh, 0:1, :]
    vec_send(DP, v0)
    vec_sum(DP, v0, v1)
    vec_send(MP, v1)
    stage_far(1)
    stage_far(0)
    vec_sum(MP, v1, v2)
    vec_send(HID, v2)
    stage_end(3)
    stage_end(2)
    stage_end(4)
    stage_end(1)
    stage_end(0)
    vec_sum(HID, v2, vecf_ref)
    for copy in held:
        copy.wait()
    for copy in moved:
        copy.wait_recv()
    wire.finish()


def backward(o, dw2, near_r, near_e, last_sum, qkv, do, lse, seg, present, ft, w1, et, dmid, cols, dbe, dbf, dgs):
    dp, mp, hid = lax.axis_size("dp"), lax.axis_size("mp"), lax.axis_size("hidden")
    sds = jax.ShapeDtypeStruct
    wide = D // hid
    half = D // mp // dp
    half2, c2 = dw2.shape[3:]
    fc = near_e.shape[3]
    ff = hid * fc
    out_shape = (
        sds((D // mp, mp * SEQ), BF16), sds((D // mp, mp * SEQ), BF16), sds((3, half, wide), F32),
        sds((half2, c2), F32), sds((half, fc), F32), sds((half, fc), F32), sds((16, D), F32),
    )
    vm = lambda *shape: pltpu.VMEM(shape, BF16)
    vf = lambda *shape: pltpu.VMEM(shape, F32)
    slabs = ((hid, mp, half, 2 * wide), (hid, mp, half, wide), (mp, hid, half2, c2))
    after = ((hid, half, 2 * wide), (mp, half, wide), (hid, half2, c2), (half, ff), (mp, half, fc))
    ends = ((half, 2 * wide), (half, wide), (half2, c2), (half, fc), (half, fc))
    near = (mp, hid, mp, mp, hid)
    far = (hid, mp, hid, hid, mp)
    scratch = [
        vm(SEQ, 3 * D), vm(SEQ, D), vf(SEQ, SEQ), vm(PAIR, SEQ), vm(D, SEQ), vm(SEQ, D), vm(SEQ, D),
        vf(SEQ, PAIR), vf(SEQ, PAIR), vm(D, SEQ), vf(D, SEQ), vf(D, SEQ), vf(2, D, 128),
    ]
    scratch += [vm(dp - 1, *s) for s in slabs]
    scratch += [vm(dp, *s) for s in slabs[:2]] + [vm(*s) for s in slabs[2:]]
    scratch += [vm(n - 1, *s) for n, s in zip(near[:3], after)] + [vm(n, *s) for n, s in zip(near[3:], after[3:])]
    scratch += [vm(*s) for s in after]
    scratch += [vm(n - 1, *s) for n, s in zip(far, ends)]
    scratch += [vf(16, D), vf(dp - 1, 16, D), vf(mp - 1, 16, D), vf(hid - 1, 16, D), vf(16, D), vf(16, D)]
    n = dp + mp + hid - 3 + 2 * mp + 4 * (dp - 1) + 1 + 6 * (mp + hid - 2)
    scratch += [pltpu.SemaphoreType.DMA((4 * PAIRS + 6 + hid,)), pltpu.SemaphoreType.DMA((n,)), pltpu.SemaphoreType.DMA((n,))]
    hbm = pl.BlockSpec(memory_space=pl.ANY)
    vmem = pl.BlockSpec(memory_space=pltpu.VMEM)
    return pl.pallas_call(
        backward_kernel,
        out_shape=out_shape,
        in_specs=[hbm] * 7 + [vmem] * 3 + [hbm] * 4 + [vmem] * 4,
        out_specs=(hbm, hbm) + (vmem,) * 5,
        scratch_shapes=scratch,
        compiler_params=params(collective_id=1, has_side_effects=True),
        name="backward",
    )(o, dw2, near_r, near_e, last_sum, qkv, do, lse, seg, present, ft, w1, et, dmid, cols, dbe, dbf, dgs)


def local(
    stored, positions, segments, present, norm_gains, norm_biases, input_proj, input_bias, output_proj,
    output_bias, expand_weight, expand_bias, reduce_weight, reduce_bias, cotangent,
):
    mp, hid, dp = lax.axis_size("mp"), lax.axis_size("hidden"), lax.axis_size("dp")
    m, h, d = lax.axis_index("mp"), lax.axis_index("hidden"), lax.axis_index("dp")
    rows_mp, hcols, fcols = D // mp, D // hid, expand_weight.shape[1]
    half = rows_mp // dp
    cols = [norm_gains[:1], norm_biases[:1], norm_gains[1:], norm_biases[1:], output_bias[None], reduce_bias[None]]
    cols = jnp.concatenate([c.astype(F32) for c in cols] + [jnp.zeros((2, rows_mp), F32)])
    cols = jnp.pad(cols, ((0, 0), (0, -rows_mp % 128)))
    rows = jnp.concatenate(
        [
            expand_bias.astype(F32)[None],
            jnp.pad(input_bias.astype(F32), ((0, 0), (0, fcols - hcols))),
            jnp.zeros((5, fcols), F32),
        ]
    )
    w1 = lax.dynamic_slice_in_dim(input_proj, d * half, half, 0)
    w2 = output_proj
    if hcols // dp % 16:
        w2 = lax.dynamic_slice_in_dim(output_proj, d * (hcols // dp), hcols // dp, 0)
    pos = positions[None]
    rate = np.exp(np.arange(D // 2, dtype=np.float32) * np.float32(-math.log(10000.0) / (D // 2)))[None]
    seg, present = segments[None], present[None]
    et, ft, w1f, qkv, out_t, dmid, do, near_r, near_e, last_sum, _, _, lse, cols, dbe, dw2, dbf, dgs = forward(
        stored, cotangent, w1[:, :2].reshape(half, 2 * hcols), w1[:, 2], w2, expand_weight, reduce_weight, cols, rows,
        pos, jnp.asarray(rate), seg, present,
    )
    output, d_stored, g1, d_output, d_expand, d_reduce, vec = backward(
        out_t,
        dw2.reshape(mp, hid, dp, hcols // dp, rows_mp),
        near_r,
        near_e,
        last_sum,
        qkv, do, lse, seg, present, ft, w1f, et, dmid, cols, dbe, dbf, dgs,
    )
    piece = D // (hid * mp * dp)
    cut = lambda x, at, size: lax.dynamic_slice_in_dim(x, at * size, size, x.ndim - 1)
    dg = cut(vec[:4].reshape(2, 2, D), (m * dp + d) * hid + h, piece)
    db_proj = cut(vec[4:6], h * dp + d, hcols // dp)
    db_feed = cut(vec[6:8], m * dp + d, half)
    dbe = cut(vec[8:].reshape(-1)[: hid * fcols], h * dp + d, fcols // dp)
    d_input = g1.transpose(1, 0, 2)
    return (
        output, d_stored.astype(F32), dg[:, 0], dg[:, 1], d_input, db_proj, d_output, db_feed[1], d_expand, dbe, d_reduce,
        db_feed[0],
    )


def solution(mesh):
    placed = (
        P("mp", ("dp", "hidden")),
        P(("dp", "hidden")),
        P(("dp", "hidden", "mp")),
        P(("dp", "hidden", "mp")),
        P(None, "mp"),
        P(None, "mp"),
        P("mp", None, "hidden"),
        P(None, "hidden"),
        P("hidden", "mp"),
        P("mp"),
        P("mp", "hidden"),
        P("hidden"),
        P("mp", "hidden"),
        P("mp"),
        P("mp", ("dp", "hidden")),
    )
    return jax.shard_map(
        local,
        mesh=mesh,
        in_specs=placed,
        out_specs=(
            P("mp", ("dp", "hidden")),
            P("mp", ("dp", "hidden")),
            P(None, ("mp", "dp", "hidden")),
            P(None, ("mp", "dp", "hidden")),
            P(("mp", "dp"), None, "hidden"),
            P(None, ("hidden", "dp")),
            P(("hidden", "dp"), "mp"),
            P(("mp", "dp")),
            P(("mp", "dp"), "hidden"),
            P(("hidden", "dp")),
            P(("mp", "dp"), "hidden"),
            P(("mp", "dp")),
        ),
        check_vma=False,
    )
```

profile of v0, /device:TPU:0, one launch (start us, length us, event | category | flops | bytes accessed | tf_op | source)
XLA Modules:
  0.0 273.2 jit_solution(3088432549123668044)
XLA Ops:
  0.6 0.0 copy-start
  0.7 0.9 copy-done
  1.6 0.1 copy.29
  1.7 0.7 reshape.39.w1a_ref
  2.5 0.6 dynamic-slice_bitcast_fusion.w1b_ref
  3.1 0.8 fusion.2
  3.9 0.7 convert_element_type.26
  4.5 0.7 convert_element_type.27
  5.2 0.6 pad.11.cols_ref
  5.8 0.7 pad_convert_fusion
  6.5 0.7 reshape.44
  7.2 0.1 pad.16.clone
  7.3 0.7 maximum_maximum_fusion.rows_ref
  7.9 157.5 %forward.1 = (f32[768,1024]{1,0:T(8,128)}, bf16[768,1024]{1,0:T(8,128)(2,1)}, bf16[768,2304]{1,0:T(8,128)(2,1)}, bf16[1024,2304]{1,0:T(8,128)(2,1)}, bf16[768,10...) custom-call(bf16[192,4096]{1,0:T(8,128)(2,1)} %x_ref.1, ...), custom_call_target="tpu_custom_call" | custom-call | tf_op jit(solution)/shard_map/forward/pallas_call | solution.py:634
  165.5 97.3 %backward.1 = (bf16[192,4096]{1,0:T(8,128)(2,1)}, bf16[192,4096]{1,0:T(8,128)(2,1)}, f32[3,96,192]{2,1,0:T(8,128)}, f32[96,192]{1,0:T(8,128)}, f32[96,768]{1,0:T...) custom-call(bf16[768,1024]{1,0:T(8,128)(2,1)} %get-tuple-element.35.o_ref, bf16[4,4,2,96,192]{4,3,2,1,0:T(8,128)(2,1)} %bitcast.19, ...), custom_call_target="tpu_custom_call" | custom-call | tf_op jit(solution)/shard_map/backward/pallas_call | solution.py:1012
  262.8 0.0 copy-start.6
  262.9 0.0 copy-start.1
  262.9 3.5 %convert_element_type.25 = f32[192,4096]{1,0:T(8,128)} convert(bf16[192,4096]{1,0:T(8,128)(2,1)} %get-tuple-element.52) | non-fusion elementwise | flops 786432 | bytes 4718592 | tf_op jit(solution)/shard_map/convert_element_type | solution.py:1068
  266.4 0.0 copy-done.6
  266.5 0.6 constant_dynamic-slice_fusion.4
  267.1 0.7 dynamic_slice.19
  267.8 0.1 constant_dynamic-slice_fusion.2
  267.9 0.5 slice_bitcast_fusion
  268.4 0.6 constant_dynamic-slice_fusion.3
  269.0 0.0 copy-done.1
  269.0 0.0 copy-start.4
  269.0 0.0 copy-start.5
  269.0 0.0 copy-start.3
  269.0 0.0 copy-start.2
  269.0 1.1 copy.39
  270.2 0.0 copy-done.4
  270.2 0.7 copy.40
  270.9 0.0 copy-done.5
  270.9 0.6 copy.41
  271.5 0.0 copy-done.3
  271.5 0.7 copy.42
  272.2 0.0 copy-done.2
  272.3 0.7 copy.43
  (8 shorter events, 0.1 us)
Async XLA Ops:
  0.6 1.0 copy-start
  262.8 3.6 %copy-start.6 = (f32[16,768]{1,0:T(8,128)S(1)}, f32[16,768]{1,0:T(8,128)}, u32[]{:S(2)}) copy-start(f32[16,768]{1,0:T(8,128)} %get-tuple-element.53) | copy-start | bytes 147460
  262.9 6.2 %copy-start.1 = (bf16[192,4096]{1,0:T(8,128)(2,1)S(1)}, bf16[192,4096]{1,0:T(8,128)(2,1)}, u32[]{:S(2)}) copy-start(bf16[192,4096]{1,0:T(8,128)(2,1)} %get-tuple-element.84) | copy-start | bytes 4718596
  269.0 1.2 copy-start.4
  269.0 1.9 copy-start.5
  269.0 2.5 copy-start.3
  269.0 3.2 %copy-start.2 = (f32[96,768]{1,0:T(8,128)S(1)}, f32[96,768]{1,0:T(8,128)}, u32[]{:S(2)}) copy-start(f32[96,768]{1,0:T(8,128)} %get-tuple-element.94) | copy-start | bytes 884740
where the time goes:
time: 277 us; the launch traced here: 273 us
  Pallas kernels  255 us (92%)
  local copies, waits for them, and re-layouts  11.1 us (4%)
  other arithmetic  6.23 us (2%)
    pallas_call x1, Pallas kernels, forward(): pl.pallas_call(forward_kernel, out_shape=out_shape, in_specs=[hbm] * 9 +...  158 us
    pallas_call x1, Pallas kernels, backward(): pl.pallas_call(backward_kernel, out_shape=out_shape, in_specs=[hbm] * 7 +...  97.3 us

commit v1 on v0

--- a/solution.py
+++ b/solution.py
@@ -200,6 +200,7 @@
             copy.wait_recv()
 
     full = (wef_ref, wrf_ref)
+    cut = tuple(ref.reshape(mp, dp, half, hid * fcols) for ref in full)
     part = (we_ref.at[pl.ds(offset, half)], wr_ref.at[pl.ds(offset, half)])
     whole_planes = ((1,), (1, hid - 1))
     order = [0, 1, hid - 1] + list(range(2, hid - 1))
@@ -218,27 +219,25 @@
         src = part[j] if o == 0 else piece(j, m, d, o)
         return remote(src, piece(j, m, d, o), (p_send.at[j, o, q], p_recv.at[j, o, q]), wire.peer(MP, q))
 
-    def to_depth(j, o, k):
+    def slab(j, o):
+        return cut[j].at[:, d, :, pl.ds(pl.multiple_of(plane_of(o) * fcols, fcols), fcols)]
+
+    def to_depth(j, o):
         if o in whole_planes[j]:
-            src = dst = piece(j, k, d, 0)
+            src = dst = slab(j, 0)
         else:
             src, dst = part[j], piece(j, m, d, 0)
-        return remote(src, dst, (z_send.at[j, o, k], z_recv.at[j, o, k]), wire.peer(HID, o))
-
-    def depth_count(j, o):
-        return mp if o in whole_planes[j] else 1
-
-    def to_core(j, o, k, r):
-        return remote(
-            piece(j, k, d, o), piece(j, k, d, o), (c_send.at[j, o, k, r - 1], c_recv.at[j, o, k, r - 1]), wire.peer(DP, r)
-        )
+        return remote(src, dst, (z_send.at[j, o], z_recv.at[j, o]), wire.peer(HID, o))
+
+    def to_core(j, o, r):
+        return remote(slab(j, o), slab(j, o), (c_send.at[j, o, r - 1], c_recv.at[j, o, r - 1]), wire.peer(DP, r))
 
     def keep_own(j):
         return pltpu.make_async_copy(part[j], piece(j, m, d, 0), local.at[j])
 
     def plane_start(j, o):
         if o:
-            to_depth(j, o, 0).wait_recv()
+            to_depth(j, o).wait_recv()
         else:
             keep_own(j).start()
         for q in range(1, mp):
@@ -251,26 +250,22 @@
             to_plane(j, o, q).wait_recv()
 
     def depth_start(j, o):
-        for k in range(depth_count(j, o)):
-            to_depth(j, o, k).start()
+        to_depth(j, o).start()
 
     def apart(j):
         return [o for o in range(1, hid) if o not in whole_planes[j]]
 
     def core_start(j, o):
         if o in whole_planes[j]:
-            for k in range(mp):
-                to_depth(j, o, k).wait_recv()
+            to_depth(j, o).wait_recv()
         elif o:
             plane_wait(j, o)
-        for k in range(mp):
-            for r in range(1, dp):
-                to_core(j, o, k, r).start()
+        for r in range(1, dp):
+            to_core(j, o, r).start()
 
     def arrived(j, o):
-        for k in range(mp):
-            for r in range(1, dp):
-                to_core(j, o, k, r).wait_recv()
+        for r in range(1, dp):
+            to_core(j, o, r).wait_recv()
 
     small = [wire.send(cols_ref, colsf.at[m], wire.peer(MP, q)) for q in range(1, mp)]
     small += [wire.send(rows_ref, rowsf.at[h], wire.peer(HID, o)) for o in range(1, hid)]
@@ -305,6 +300,11 @@
         wb[:, hh * wide : (hh + 1) * wide] = rowsf[hh, 1:2, :wide]
         wb[:, 2 * D + hh * wide : 2 * D + (hh + 1) * wide] = rowsf[hh, 2:3, :wide]
     landed(x_in)
+    plane_start(1, 0)
+    for j in (1, 0):
+        for o in apart(j):
+            depth_start(j, o)
+    stage_one(2)
 
     def norm_cols(j, _):
         cols = pl.ds(pl.multiple_of(j * 256, 256), 256)
@@ -320,11 +320,6 @@
     stored += [wire.keep(et, et_out), wire.keep(ft, ft_out)]
     stage_three(0)
     stage_three(1)
-    for j in (1, 0):
-        for o in apart(j):
-            depth_start(j, o)
-    plane_start(1, 0)
-    stage_one(2)
     plane_start(0, 0)
     c_in = swap(c_ref, ct)
     def unpack(dd):
@@ -445,17 +440,16 @@
             o = jnp.where(n == k, order[k], o)
         return o
 
-    def swap_core(j, n, k, r):
+    def swap_core(j, n, r):
         to = wire.peer(DP, r)
         return remote(
-            dblk.at[j, k, to[0]], theirs.at[lax.rem(n, 2), j, r - 1, k], (x_send.at[j, n, k, r - 1], x_recv.at[j, n, k, r - 1]), to
+            dblk.at[j, :, to[0]], theirs.at[lax.rem(n, 2), j, r - 1], (x_send.at[j, n, r - 1], x_recv.at[j, n, r - 1]), to
         )
 
     def each_core(n, do):
         for j in range(2):
-            for k in range(mp):
-                for r in range(1, dp):
-                    do(swap_core(j, n, k, r))
+            for r in range(1, dp):
+                do(swap_core(j, n, r))
 
     end = hid - 1
 
@@ -603,14 +597,12 @@
     for j in range(2):
         for o in range(hid):
             if o:
-                for k in range(depth_count(j, o)):
-                    to_depth(j, o, k).wait_send()
+                to_depth(j, o).wait_send()
             if o not in whole_planes[j]:
                 for q in range(1, mp):
                     to_plane(j, o, q).wait_send()
-            for k in range(mp):
-                for r in range(1, dp):
-                    to_core(j, o, k, r).wait_send()
+            for r in range(1, dp):
+                to_core(j, o, r).wait_send()
 
 
 def forward(x, c, w1a, w1b, w2, we, wr, cols, rows, pos, rate, seg, present):
@@ -644,8 +636,8 @@
             vm(BF16, SEQ, 3 * D), vm(F32, SEQ, SEQ), vm(BF16, PAIR, SEQ), vm(F32, 1, 3 * D),
             vm(BF16, D, SEQ), vm(BF16, D, SEQ), vm(BF16, 2, D, fc), vm(BF16, 2, mp, dp, half, fc), vm(BF16, D, D),
             vm(BF16, 2, 2, dp - 1, mp, half, fc), vm(BF16, 2, 2, mp, half, fc),
-            sem(n), sem(n), sem(2, hid, mp), sem(2, hid, mp), sem(2, hid, mp), sem(2, hid, mp),
-            sem(2, hid, mp, dp - 1), sem(2, hid, mp, dp - 1), sem(2, hid, mp, dp - 1), sem(2, hid, mp, dp - 1),
+            sem(n), sem(n), sem(2, hid), sem(2, hid), sem(2, hid, mp), sem(2, hid, mp),
+            sem(2, hid, dp - 1), sem(2, hid, dp - 1), sem(2, hid, dp - 1), sem(2, hid, dp - 1),
             sem(hid, mp), sem(hid, mp), sem(2, hid), sem(4),
         ],
         compiler_params=params(collective_id=0, has_side_effects=True),

time: 277 us -> 274 us (0.989)
  Pallas kernels: 255 us -> 251 us
    pallas_call x1, Pallas kernels: 158 us -> 152 us  [forward(): pl.pallas_call(forward_kernel, out_shape=out_shape, in_specs=[hbm] * 9 +...]
where the time goes in v1:
time: 274 us; the launch traced here: 269 us
  Pallas kernels  251 us (92%)
  local copies, waits for them, and re-layouts  11.1 us (4%)
  other arithmetic  6.23 us (2%)
    pallas_call x1, Pallas kernels, forward(): pl.pallas_call(forward_kernel, out_shape=out_shape, in_specs=[hbm] * 9 +...  152 us
    pallas_call x1, Pallas kernels, backward(): pl.pallas_call(backward_kernel, out_shape=out_shape, in_specs=[hbm] * 7 +...  98.4 us

profile of v1, /device:TPU:0, one launch (start us, length us, event | category | flops | bytes accessed | tf_op | source)
XLA Modules:
  0.0 269.4 jit_solution(16498419356983831263)
XLA Ops:
  0.6 0.0 copy-start
  0.7 0.9 copy-done
  1.6 0.1 copy.29
  1.7 0.7 reshape.39.w1a_ref
  2.5 0.6 dynamic-slice_bitcast_fusion.w1b_ref
  3.1 0.8 fusion.2
  3.9 0.7 convert_element_type.26
  4.5 0.7 convert_element_type.27
  5.2 0.6 pad.11.cols_ref
  5.8 0.7 pad_convert_fusion
  6.5 0.7 reshape.44
  7.2 0.1 pad.16.clone
  7.3 0.7 maximum_maximum_fusion.rows_ref
  7.9 152.5 %forward.1 = (f32[768,1024]{1,0:T(8,128)}, bf16[768,1024]{1,0:T(8,128)(2,1)}, bf16[768,2304]{1,0:T(8,128)(2,1)}, bf16[1024,2304]{1,0:T(8,128)(2,1)}, bf16[768,10...) custom-call(bf16[192,4096]{1,0:T(8,128)(2,1)} %x_ref.1, ...), custom_call_target="tpu_custom_call" | custom-call | tf_op jit(solution)/shard_map/forward/pallas_call | solution.py:626
  160.4 98.4 %backward.1 = (bf16[192,4096]{1,0:T(8,128)(2,1)}, bf16[192,4096]{1,0:T(8,128)(2,1)}, f32[3,96,192]{2,1,0:T(8,128)}, f32[96,192]{1,0:T(8,128)}, f32[96,768]{1,0:T...) custom-call(bf16[768,1024]{1,0:T(8,128)(2,1)} %get-tuple-element.35.o_ref, bf16[4,4,2,96,192]{4,3,2,1,0:T(8,128)(2,1)} %bitcast.19, ...), custom_call_target="tpu_custom_call" | custom-call | tf_op jit(solution)/shard_map/backward/pallas_call | solution.py:1004
  258.8 0.0 copy-start.6
  258.8 0.0 copy-start.1
  258.9 3.5 %convert_element_type.25 = f32[192,4096]{1,0:T(8,128)} convert(bf16[192,4096]{1,0:T(8,128)(2,1)} %get-tuple-element.52) | non-fusion elementwise | flops 786432 | bytes 4718592 | tf_op jit(solution)/shard_map/convert_element_type | solution.py:1060
  262.4 0.0 copy-done.6
  262.4 0.6 constant_dynamic-slice_fusion.4
  263.1 0.7 dynamic_slice.19
  263.8 0.1 constant_dynamic-slice_fusion.2
  263.8 0.5 slice_bitcast_fusion
  264.4 0.6 constant_dynamic-slice_fusion.3
  265.0 0.0 copy-done.1
  265.0 0.0 copy-start.4
  265.0 0.0 copy-start.5
  265.0 0.0 copy-start.3
  265.0 0.0 copy-start.2
  265.0 1.1 copy.39
  266.2 0.0 copy-done.4
  266.2 0.7 copy.40
  266.9 0.0 copy-done.5
  266.9 0.6 copy.41
  267.5 0.0 copy-done.3
  267.5 0.7 copy.42
  268.2 0.0 copy-done.2
  268.2 0.7 copy.43
  (8 shorter events, 0.1 us)
Async XLA Ops:
  0.6 1.0 copy-start
  258.8 3.6 %copy-start.6 = (f32[16,768]{1,0:T(8,128)S(1)}, f32[16,768]{1,0:T(8,128)}, u32[]{:S(2)}) copy-start(f32[16,768]{1,0:T(8,128)} %get-tuple-element.53) | copy-start | bytes 147460
  258.8 6.2 %copy-start.1 = (bf16[192,4096]{1,0:T(8,128)(2,1)S(1)}, bf16[192,4096]{1,0:T(8,128)(2,1)}, u32[]{:S(2)}) copy-start(bf16[192,4096]{1,0:T(8,128)(2,1)} %get-tuple-element.84) | copy-start | bytes 4718596
  265.0 1.2 copy-start.4
  265.0 1.9 copy-start.5
  265.0 2.5 copy-start.3
  265.0 3.2 %copy-start.2 = (f32[96,768]{1,0:T(8,128)S(1)}, f32[96,768]{1,0:T(8,128)}, u32[]{:S(2)}) copy-start(f32[96,768]{1,0:T(8,128)} %get-tuple-element.94) | copy-start | bytes 884740

commit v2 on v1

--- a/solution.py
+++ b/solution.py
@@ -914,9 +914,10 @@
         df[:, cols] = value
         return 0
 
-    lax.fori_loop(0, SEQ // 256, feature_cols, 0)
+    lax.fori_loop(0, SEQ // 512, feature_cols, 0)
     stage_near(1)
     near_half(1)
+    lax.fori_loop(SEQ // 512, SEQ // 256, feature_cols, 0)
     dgp[...] = jnp.zeros_like(dgp)
 
     def norm_cols(j, _):
@@ -949,10 +950,10 @@
         row, lane = divmod(hh * fcols, D)
         v0[8 + row : 9 + row, lane : lane + fcols] = dbe_ref[hh, 0:1, :]
     vec_send(DP, v0)
+    stage_far(0)
     vec_sum(DP, v0, v1)
     vec_send(MP, v1)
     stage_far(1)
-    stage_far(0)
     vec_sum(MP, v1, v2)
     vec_send(HID, v2)
     stage_end(3)

time: 274 us -> 271 us (0.989)
  no operation moved by 1% of the time
where the time goes in v2:
time: 271 us; the launch traced here: 267 us
  Pallas kernels  249 us (92%)
  local copies, waits for them, and re-layouts  11.1 us (4%)
  other arithmetic  6.23 us (2%)
    pallas_call x1, Pallas kernels, forward(): pl.pallas_call(forward_kernel, out_shape=out_shape, in_specs=[hbm] * 9 +...  152 us
    pallas_call x1, Pallas kernels, backward(): pl.pallas_call(backward_kernel, out_shape=out_shape, in_specs=[hbm] * 7 +...  96.3 us

profile of v2, /device:TPU:0, one launch (start us, length us, event | category | flops | bytes accessed | tf_op | source)
XLA Modules:
  0.0 267.3 jit_solution(9340427855362928227)
XLA Ops:
  0.6 0.0 copy-start
  0.7 0.9 copy-done
  1.6 0.1 copy.29
  1.7 0.7 reshape.39.w1a_ref
  2.5 0.6 dynamic-slice_bitcast_fusion.w1b_ref
  3.1 0.8 fusion.2
  3.9 0.7 convert_element_type.26
  4.5 0.7 convert_element_type.27
  5.2 0.6 pad.11.cols_ref
  5.8 0.7 pad_convert_fusion
  6.5 0.7 reshape.44
  7.2 0.1 pad.16.clone
  7.3 0.7 maximum_maximum_fusion.rows_ref
  7.9 152.5 %forward.1 = (f32[768,1024]{1,0:T(8,128)}, bf16[768,1024]{1,0:T(8,128)(2,1)}, bf16[768,2304]{1,0:T(8,128)(2,1)}, bf16[1024,2304]{1,0:T(8,128)(2,1)}, bf16[768,10...) custom-call(bf16[192,4096]{1,0:T(8,128)(2,1)} %x_ref.1, ...), custom_call_target="tpu_custom_call" | custom-call | tf_op jit(solution)/shard_map/forward/pallas_call | solution.py:626
  160.4 96.3 %backward.1 = (bf16[192,4096]{1,0:T(8,128)(2,1)}, bf16[192,4096]{1,0:T(8,128)(2,1)}, f32[3,96,192]{2,1,0:T(8,128)}, f32[96,192]{1,0:T(8,128)}, f32[96,768]{1,0:T...) custom-call(bf16[768,1024]{1,0:T(8,128)(2,1)} %get-tuple-element.35.o_ref, bf16[4,4,2,96,192]{4,3,2,1,0:T(8,128)(2,1)} %bitcast.19, ...), custom_call_target="tpu_custom_call" | custom-call | tf_op jit(solution)/shard_map/backward/pallas_call | solution.py:1005
  256.7 0.0 copy-start.6
  256.7 0.0 copy-start.1
  256.7 3.5 %convert_element_type.25 = f32[192,4096]{1,0:T(8,128)} convert(bf16[192,4096]{1,0:T(8,128)(2,1)} %get-tuple-element.52) | non-fusion elementwise | flops 786432 | bytes 4718592 | tf_op jit(solution)/shard_map/convert_element_type | solution.py:1061
  260.3 0.0 copy-done.6
  260.3 0.6 constant_dynamic-slice_fusion.4
  261.0 0.7 dynamic_slice.19
  261.7 0.1 constant_dynamic-slice_fusion.2
  261.7 0.5 slice_bitcast_fusion
  262.3 0.6 constant_dynamic-slice_fusion.3
  262.9 0.0 copy-done.1
  262.9 0.0 copy-start.4
  262.9 0.0 copy-start.5
  262.9 0.0 copy-start.3
  262.9 0.0 copy-start.2
  262.9 1.1 copy.39
  264.1 0.0 copy-done.4
  264.1 0.7 copy.40
  264.8 0.0 copy-done.5
  264.8 0.6 copy.41
  265.4 0.0 copy-done.3
  265.4 0.7 copy.42
  266.1 0.0 copy-done.2
  266.1 0.7 copy.43
  (8 shorter events, 0.1 us)
Async XLA Ops:
  0.6 1.0 copy-start
  256.7 3.6 %copy-start.6 = (f32[16,768]{1,0:T(8,128)S(1)}, f32[16,768]{1,0:T(8,128)}, u32[]{:S(2)}) copy-start(f32[16,768]{1,0:T(8,128)} %get-tuple-element.53) | copy-start | bytes 147460
  256.7 6.2 %copy-start.1 = (bf16[192,4096]{1,0:T(8,128)(2,1)S(1)}, bf16[192,4096]{1,0:T(8,128)(2,1)}, u32[]{:S(2)}) copy-start(bf16[192,4096]{1,0:T(8,128)(2,1)} %get-tuple-element.84) | copy-start | bytes 4718596
  262.9 1.2 copy-start.4
  262.9 1.9 copy-start.5
  262.9 2.5 copy-start.3
  262.9 3.2 %copy-start.2 = (f32[96,768]{1,0:T(8,128)S(1)}, f32[96,768]{1,0:T(8,128)}, u32[]{:S(2)}) copy-start(f32[96,768]{1,0:T(8,128)} %get-tuple-element.94) | copy-start | bytes 884740
